TPU v7x, 32 devices: a whole 2x2x4 slice. The times are simulated.
32 devices in a mesh: groups: 2 (over x), dp: 16 (over z, y, core).
Axes of the slice: x: 2, y: 2, z: 4, core: 2. Of those that a mesh axis runs over, the one named last changes fastest.
Arguments:
- wave: float32 [2048, 320], P(('groups', 'dp')), parts along dimension 0, may hold values from -7.5 to 7.5
- row_slot: int32 [2048], P(('groups', 'dp')), parts along dimension 0, may hold values from 0 to 1023, as said below
- frame_lengths: int32 [128], P('groups'), parts along dimension 0, may hold values from 1 to 256, 1024 in all
- sample_trim: int32 [128], P('groups'), parts along dimension 0, may hold values from 0 to 319
- first_weight: float32 [10, 512], replicated, may hold values from -2 to 2
- mid_weight: bfloat16 [4, 3, 512, 512], replicated, may hold values from -0.15625 to 0.15625
- tail_weight: bfloat16 [2, 2, 512, 512], replicated, may hold values from -0.1875 to 0.1875
Outputs:
- centered: bfloat16 [2048, 512], P(('groups', 'dp')), parts along dimension 0
There are 2 independent parts, one for each index of `groups`. A program takes and returns all parts, laid end to end along the dimension named above; an argument that names none is the same for every part. Nothing has to cross between parts.
Inputs may be any that keep to these rules, and one draw needn't show every extreme that they name: row_slot is a permutation of 0 .. 1023. For every index h of dp and every index o, at most 6 of the 64 rows of h have row_slot in [o * 64, (o + 1) * 64), and for every h exactly one o receives 6 of them. frame_lengths sum to 1024, and the largest is 256.
All inputs are finite; a program needn't handle non-finite values.
Results may differ from a plain program's by a relative error of at most 0.023.
Values sent between devices are 32-bit elements; how exact they have to be, the bound alone decides.
A program may use at most 64 MiB of HBM per device.

v0:
```python
import jax
import jax.numpy as jnp
from jax import lax
from jax.sharding import PartitionSpec as P

BLOCK = 320
LOOK = 80
MID = 4
TAIL = 2
MAXLEN = 256


def from_behind(value, axis, steps):
    count = lax.axis_size(axis)
    initial, last = (max(0, -steps), min(count, count - steps))
    return lax.ppermute(value, axis, [(source, source + steps) for source in range(initial, last)])


def norm_gelu(values):
    average = jnp.mean(values, axis=-1, keepdims=True)
    centred = values - average
    spread = jnp.mean(centred * centred, axis=-1, keepdims=True)
    return jax.nn.gelu(centred / jnp.sqrt(spread + 1e-05), approximate=False).astype(jnp.bfloat16)


def strided(inputs, weight, stride):
    kernel = weight.shape[0]
    length = (inputs.shape[0] - kernel) // stride + 1
    summed = jnp.zeros((length, weight.shape[2]), jnp.float32)
    for offset in range(kernel):
        shifted = lax.slice_in_dim(inputs, offset, offset + stride * (length - 1) + 1, stride, 0)
        summed = summed + jnp.dot(shifted, weight[offset], preferred_element_type=jnp.float32)
    return summed


def first_layer(samples, first_weight):
    fifths = samples.reshape(-1, 5)
    patches = jnp.concatenate([fifths[:-1], fifths[1:]], axis=1)
    return norm_gelu(
        jnp.dot(
            patches,
            first_weight,
            precision=lax.Precision.HIGHEST,
            preferred_element_type=jnp.float32,
        )
    )


def per_device(wave, row_slot, frame_lengths, sample_trim, first_weight, mid_weight, tail_weight):
    rows_here = wave.shape[0]
    devices = lax.axis_size("dp")
    capacity = rows_here // devices + 2
    device = lax.axis_index("dp")
    target = row_slot // rows_here
    chosen = (target[:, None] == jnp.arange(devices, dtype=jnp.int32)[None, :]).astype(jnp.int32)
    earlier_rows = jnp.sum((jnp.cumsum(chosen, axis=0) - chosen) * chosen, axis=1)
    slot_index = target * capacity + earlier_rows
    send_rows = jnp.zeros((devices * capacity, BLOCK), jnp.float32).at[slot_index].set(wave)
    send_slots = jnp.full((devices * capacity,), -1, jnp.int32).at[slot_index].set(row_slot)
    got_rows, got_slots = (
        lax.all_to_all(send_rows, "dp", split_axis=0, concat_axis=0, tiled=True),
        lax.all_to_all(send_slots, "dp", split_axis=0, concat_axis=0, tiled=True),
    )
    landing = jnp.where(got_slots >= 0, got_slots - device * rows_here, rows_here)
    stream = jnp.zeros((rows_here, BLOCK), jnp.float32).at[landing].set(got_rows, mode="drop")
    frame_ids = device * rows_here + jnp.arange(rows_here, dtype=jnp.int32)
    starts = jnp.cumsum(frame_lengths) - frame_lengths
    member = (starts[None, :] <= frame_ids[:, None]) & (
        frame_ids[:, None] < (starts + frame_lengths)[None, :]
    )
    member_int = member.astype(jnp.int32)
    start_here = jnp.sum(member_int * starts[None, :], axis=1)
    limit_here = jnp.sum(member_int * (BLOCK * frame_lengths - sample_trim)[None, :], axis=1)
    within = ((frame_ids - start_here) * BLOCK)[:, None] + jnp.arange(BLOCK, dtype=jnp.int32)[
        None, :
    ]
    signal = jnp.where(within < limit_here[:, None], stream, 0.0).reshape(-1)
    following = from_behind(signal[:LOOK], "dp", -1)
    samples = jnp.concatenate([signal, following])
    hidden = first_layer(samples, first_weight)
    for step_index in range(MID):
        hidden = norm_gelu(strided(hidden, mid_weight[step_index], 2))
    for step_index in range(TAIL):
        hidden = norm_gelu(strided(hidden, tail_weight[step_index], 2))
    rollouts = frame_lengths.shape[0]
    local_sums = lax.dot_general(
        member.astype(jnp.bfloat16),
        hidden,
        (((0,), (0,)), ((), ())),
        preferred_element_type=jnp.float32,
    )
    rollout_ids = jnp.sum(member_int * jnp.arange(rollouts, dtype=jnp.int32)[None, :], axis=1)
    first_id = rollout_ids[0]
    last_id = rollout_ids[rows_here - 1]
    first_row = lax.dynamic_index_in_dim(local_sums, first_id, 0, keepdims=False)
    last_row = lax.dynamic_index_in_dim(local_sums, last_id, 0, keepdims=False)
    first_float = first_id.astype(jnp.float32)
    last_float = last_id.astype(jnp.float32)
    reach = min((MAXLEN + rows_here - 2) // rows_here + 1, devices - 1)
    add_low = jnp.zeros_like(first_row)
    add_high = jnp.zeros_like(last_row)
    for distance in range(1, reach + 1):
        below_id, below_row = from_behind((last_float + 1.0, last_row), "dp", distance)
        above_id, above_row = from_behind((first_float + 1.0, first_row), "dp", -distance)
        add_low = add_low + jnp.where(below_id == first_float + 1.0, below_row, 0.0)
        add_high = add_high + jnp.where(above_id == last_float + 1.0, above_row, 0.0)
    totals = local_sums.at[first_id].add(add_low).at[last_id].add(add_high)
    rollout_mean = totals / frame_lengths[:, None].astype(jnp.float32)
    mean_rows = jnp.dot(
        member.astype(jnp.float32),
        rollout_mean,
        precision=lax.Precision.HIGHEST,
        preferred_element_type=jnp.float32,
    )
    return (hidden.astype(jnp.float32) - mean_rows).astype(jnp.bfloat16)


def solution(mesh):
    placed = (
        P(("groups", "dp"), None),
        P(("groups", "dp")),
        P("groups"),
        P("groups"),
        P(),
        P(),
        P(),
    )
    return jax.shard_map(
        per_device, mesh=mesh, in_specs=placed, out_specs=P(("groups", "dp"), None), check_vma=False
    )
```

profile of v0, /device:TPU:11, one launch (start us, length us, event | category | flops | bytes accessed | tf_op | source)
XLA Modules:
  0.0 277.7 jit_solution(10213457404326371199)
XLA Ops:
  3.3 4.4 %collective-permute-start.1 = (f32[]{:T(128)}, f32[]{:T(128)}, u32[]{:S(2)}, u32[]{:S(2)}) collective-permute-start(f32[]{:T(128)} %add.257), channel_id=1, source_target_pairs={{0,1},{1,2},{2,3},{3,4},{4,5},{5,6},{6,7},{7,8},{8,9},{9,10},{10,1... | collective-permute-start | bytes 20 | tf_op jit(solution)/shard_map/ppermute | solution.py:16
  7.7 3.8 %collective-permute-start.3 = (f32[]{:T(128)}, f32[]{:T(128)}, u32[]{:S(2)}, u32[]{:S(2)}) collective-permute-start(f32[]{:T(128)} %add.257), channel_id=1, source_target_pairs={{0,2},{1,3},{2,4},{3,5},{4,6},{5,7},{6,8},{7,9},{8,10},{9,11},{10,... | collective-permute-start | bytes 20 | tf_op jit(solution)/shard_map/ppermute | solution.py:16
  11.5 3.6 %collective-permute-start.5 = (f32[]{:T(128)}, f32[]{:T(128)}, u32[]{:S(2)}, u32[]{:S(2)}) collective-permute-start(f32[]{:T(128)} %add.257), channel_id=1, source_target_pairs={{0,3},{1,4},{2,5},{3,6},{4,7},{5,8},{6,9},{7,10},{8,11},{9,12},{10... | collective-permute-start | bytes 20 | tf_op jit(solution)/shard_map/ppermute | solution.py:16
  15.2 3.9 %collective-permute-start.7 = (f32[]{:T(128)}, f32[]{:T(128)}, u32[]{:S(2)}, u32[]{:S(2)}) collective-permute-start(f32[]{:T(128)} %add.257), channel_id=1, source_target_pairs={{0,4},{1,5},{2,6},{3,7},{4,8},{5,9},{6,10},{7,11},{8,12},{9,13},{1... | collective-permute-start | bytes 20 | tf_op jit(solution)/shard_map/ppermute | solution.py:16
  22.4 5.4 %all-to-all-start = ((s32[16,6,1]{1,2,0:T(1,128)}), s32[16,6,1]{1,2,0:T(1,128)S(1)}, u32[]{:S(2)}, u32[]{:S(2)}) async-start(s32[16,6,1]{1,2,0:T(1,128)} %bitcast.1), calls=%async_computation | async-start | bytes 16384 | tf_op jit(solution)/shard_map/all_to_all | solution.py:62
  33.5 6.1 %all-to-all-start.1 = ((f32[16,6,320]{2,1,0:T(8,128)}), f32[16,6,320]{2,1,0:T(8,128)S(1)}, u32[]{:S(2)}, u32[]{:S(2)}) async-start(f32[16,6,320]{2,1,0:T(8,128)} %all_to_all.16), calls=%async_computation.1 | async-start | bytes 393216 | tf_op jit(solution)/shard_map/all_to_all | solution.py:61
  39.8 7.2 %all-to-all-done.1 = f32[16,6,320]{2,1,0:T(8,128)S(1)} async-done(((f32[16,6,320]{2,1,0:T(8,128)}), f32[16,6,320]{2,1,0:T(8,128)S(1)}, u32[]{:S(2)}, u32[]{:S(2)}) %all-to-all-start.1) | async-done | bytes 122912 | tf_op jit(solution)/shard_map/all_to_all | solution.py:61
  50.1 2.9 %collective-permute-done = f32[80]{0:T(128)S(1)} collective-permute-done((f32[80]{0:T(128)S(1)}, f32[80]{0:T(128)S(1)}, u32[]{:S(2)}, u32[]{:S(2)}) %collective-permute-start) | collective-permute-done | bytes 352 | tf_op jit(solution)/shard_map/ppermute | solution.py:16
  61.0 7.0 %fusion.130 = (f32[4111]{0:T(1024)S(1)}, f32[4111,512]{1,0:T(8,128)S(1)}) fusion(f32[10,512]{1,0:T(8,128)S(1)} %copy-done, f32[4111,5]{0,1:T(8,128)S(1)} %copy.17, f32[4111,5]{0,1:T(8,128)S(1)} %copy.16), kind=kOutput, calls=%fused_computation.257 | convolution fusion | flops 254721664 | bytes 8620692 | tf_op jit(solution)/shard_map/dot_general | solution.py:40
  69.7 23.6 %fusion.2 = bf16[4111,512]{1,0:T(8,128)(2,1)} fusion(f32[4111,512]{1,0:T(8,128)S(1)} %get-tuple-element.44, f32[4111]{0:T(1024)S(1)} %add_sqrt_fusion, f32[4111]{0:T(1024)S(1)} %broadcast_multiply_fusion), kind=kLoop, calls=%fused_computation.6 | loop fusion | flops 141023744 | bytes 12661880 | tf_op jit(solution)/shard_map/convert_element_type | solution.py:23
  93.3 20.5 %slice.204 = bf16[2055,512]{1,0:T(8,128)(2,1)} slice(bf16[4111,512]{1,0:T(8,128)(2,1)} %fusion.2), slice={[0:4109:2], [0:512:1]} | slice | bytes 4208640 | tf_op jit(solution)/shard_map/slice | solution.py:31
  113.8 20.5 %slice.206 = bf16[2055,512]{1,0:T(8,128)(2,1)} slice(bf16[4111,512]{1,0:T(8,128)(2,1)} %fusion.2), slice={[1:4110:2], [0:512:1]} | slice | bytes 4208640 | tf_op jit(solution)/shard_map/slice | solution.py:31
  134.3 19.0 %slice.208 = bf16[2055,512]{1,0:T(8,128)(2,1)S(1)} slice(bf16[4111,512]{1,0:T(8,128)(2,1)} %fusion.2), slice={[2:4111:2], [0:512:1]} | slice | bytes 4208640 | tf_op jit(solution)/shard_map/slice | solution.py:31
  153.3 3.1 %fusion.64 = f32[2055,512]{1,0:T(8,128)S(1)} fusion(bf16[2055,512]{1,0:T(8,128)(2,1)} %slice.204, bf16[4,3,512,512]{3,2,1,0:T(8,128)(2,1)} %param.16), kind=kOutput, calls=%fused_computation.119 | convolution fusion | flops 1077411840 | bytes 6838272 | tf_op jit(solution)/shard_map/dot_general | solution.py:32
  162.3 11.3 %fusion.12 = bf16[2055,512]{1,0:T(8,128)(2,1)S(1)} fusion(f32[2055,512]{1,0:T(8,128)S(1)} %get-tuple-element.46, f32[2055]{0:T(1024)S(1)} %add_sqrt_fusion.1, f32[2055]{0:T(1024)S(1)} %broadcast_multiply_fusion.1), kind=kLoop, calls=%fused_computation.28 | loop fusion | flops 70494720 | bytes 6329400 | tf_op jit(solution)/shard_map/convert_element_type | solution.py:23
  175.6 6.8 %slice.212 = bf16[1027,512]{1,0:T(8,128)(2,1)} slice(bf16[2055,512]{1,0:T(8,128)(2,1)S(1)} %fusion.12), slice={[1:2054:2], [0:512:1]} | slice | bytes 2103296 | tf_op jit(solution)/shard_map/slice | solution.py:31
  182.4 6.9 %slice.214 = bf16[1027,512]{1,0:T(8,128)(2,1)} slice(bf16[2055,512]{1,0:T(8,128)(2,1)S(1)} %fusion.12), slice={[2:2055:2], [0:512:1]} | slice | bytes 2103296 | tf_op jit(solution)/shard_map/slice | solution.py:31
  195.5 5.7 %fusion.22 = bf16[1027,512]{1,0:T(8,128)(2,1)S(1)} fusion(f32[1027,512]{1,0:T(8,128)S(1)} %get-tuple-element.48, f32[1027]{0:T(1024)S(1)} %add_sqrt_fusion.2, f32[1027]{0:T(1024)S(1)} %broadcast_multiply_fusion.2), kind=kLoop, calls=%fused_computation.50 | loop fusion | flops 35230208 | bytes 3163160 | tf_op jit(solution)/shard_map/convert_element_type | solution.py:23
  209.7 3.0 %fusion.33 = bf16[513,512]{1,0:T(8,128)(2,1)S(1)} fusion(f32[513,512]{1,0:T(8,128)S(1)} %get-tuple-element.50, f32[513]{0:T(1024)S(1)} %add_sqrt_fusion.3, f32[513]{0:T(1024)S(1)} %broadcast_multiply_fusion.3), kind=kLoop, calls=%fused_computation.78 | loop fusion | flops 17597952 | bytes 1580040 | tf_op jit(solution)/shard_map/convert_element_type | solution.py:23
  226.9 3.7 %collective-permute-start.2 = (f32[512]{0:T(512)S(1)}, f32[512]{0:T(512)S(1)}, u32[]{:S(2)}, u32[]{:S(2)}) collective-permute-start(f32[512]{0:T(512)S(1)} %bitcast.94), channel_id=1, source_target_pairs={{0,1},{1,2},{2,3},{3,4},{4,5},{5,6},{6,7},{7,8},{8,9},{9,10},{10,1... | collective-permute-start | bytes 6152 | tf_op jit(solution)/shard_map/ppermute | solution.py:16
  242.1 3.2 %collective-permute-start.11 = (f32[]{:T(128)}, f32[]{:T(128)}, u32[]{:S(2)}, u32[]{:S(2)}) collective-permute-start(f32[]{:T(128)} %add.258), channel_id=1, source_target_pairs={{1,0},{2,1},{3,2},{4,3},{5,4},{6,5},{7,6},{8,7},{9,8},{10,9},{11,1... | collective-permute-start | bytes 20 | tf_op jit(solution)/shard_map/ppermute | solution.py:16
  245.3 4.3 %collective-permute-start.13 = (f32[]{:T(128)}, f32[]{:T(128)}, u32[]{:S(2)}, u32[]{:S(2)}) collective-permute-start(f32[]{:T(128)} %add.258), channel_id=1, source_target_pairs={{2,0},{3,1},{4,2},{5,3},{6,4},{7,5},{8,6},{9,7},{10,8},{11,9},{12,... | collective-permute-start | bytes 20 | tf_op jit(solution)/shard_map/ppermute | solution.py:16
  249.7 4.3 %collective-permute-start.15 = (f32[]{:T(128)}, f32[]{:T(128)}, u32[]{:S(2)}, u32[]{:S(2)}) collective-permute-start(f32[]{:T(128)} %add.258), channel_id=1, source_target_pairs={{3,0},{4,1},{5,2},{6,3},{7,4},{8,5},{9,6},{10,7},{11,8},{12,9},{13... | collective-permute-start | bytes 20 | tf_op jit(solution)/shard_map/ppermute | solution.py:16
  273.0 3.0 %collective-permute-done.20 = f32[512]{0:T(512)S(1)} collective-permute-done((f32[512]{0:T(512)S(1)}, f32[512]{0:T(512)S(1)}, u32[]{:S(2)}, u32[]{:S(2)}) %collective-permute-start.20) | collective-permute-done | bytes 2080 | tf_op jit(solution)/shard_map/ppermute | solution.py:16
  (139 shorter events, 82.0 us)
Async XLA Ops:
  0.0 61.0 %copy-start = (f32[10,512]{1,0:T(8,128)S(1)}, f32[10,512]{1,0:T(8,128)}, u32[]{:S(2)}) copy-start(f32[10,512]{1,0:T(8,128)} %param.15) | copy-start | bytes 61444
  3.3 221.2 %collective-permute-start.1 = (f32[]{:T(128)}, f32[]{:T(128)}, u32[]{:S(2)}, u32[]{:S(2)}) collective-permute-start(f32[]{:T(128)} %add.257), channel_id=1, source_target_pairs={{0,1},{1,2},{2,3},{3,4},{4,5},{5,6},{6,7},{7,8},{8,9},{9,10},{10,1... | collective-permute-start | bytes 20 | tf_op jit(solution)/shard_map/ppermute | solution.py:16
  7.7 219.2 %collective-permute-start.3 = (f32[]{:T(128)}, f32[]{:T(128)}, u32[]{:S(2)}, u32[]{:S(2)}) collective-permute-start(f32[]{:T(128)} %add.257), channel_id=1, source_target_pairs={{0,2},{1,3},{2,4},{3,5},{4,6},{5,7},{6,8},{7,9},{8,10},{9,11},{10,... | collective-permute-start | bytes 20 | tf_op jit(solution)/shard_map/ppermute | solution.py:16
  11.5 219.1 %collective-permute-start.5 = (f32[]{:T(128)}, f32[]{:T(128)}, u32[]{:S(2)}, u32[]{:S(2)}) collective-permute-start(f32[]{:T(128)} %add.257), channel_id=1, source_target_pairs={{0,3},{1,4},{2,5},{3,6},{4,7},{5,8},{6,9},{7,10},{8,11},{9,12},{10... | collective-permute-start | bytes 20 | tf_op jit(solution)/shard_map/ppermute | solution.py:16
  15.2 218.4 %collective-permute-start.7 = (f32[]{:T(128)}, f32[]{:T(128)}, u32[]{:S(2)}, u32[]{:S(2)}) collective-permute-start(f32[]{:T(128)} %add.257), channel_id=1, source_target_pairs={{0,4},{1,5},{2,6},{3,7},{4,8},{5,9},{6,10},{7,11},{8,12},{9,13},{1... | collective-permute-start | bytes 20 | tf_op jit(solution)/shard_map/ppermute | solution.py:16
  22.4 11.2 %all-to-all-start = ((s32[16,6,1]{1,2,0:T(1,128)}), s32[16,6,1]{1,2,0:T(1,128)S(1)}, u32[]{:S(2)}, u32[]{:S(2)}) async-start(s32[16,6,1]{1,2,0:T(1,128)} %bitcast.1), calls=%async_computation | async-start | bytes 16384 | tf_op jit(solution)/shard_map/all_to_all | solution.py:62
  33.5 13.4 %all-to-all-start.1 = ((f32[16,6,320]{2,1,0:T(8,128)}), f32[16,6,320]{2,1,0:T(8,128)S(1)}, u32[]{:S(2)}, u32[]{:S(2)}) async-start(f32[16,6,320]{2,1,0:T(8,128)} %all_to_all.16), calls=%async_computation.1 | async-start | bytes 393216 | tf_op jit(solution)/shard_map/all_to_all | solution.py:61
  48.1 4.9 %collective-permute-start = (f32[80]{0:T(128)S(1)}, f32[80]{0:T(128)S(1)}, u32[]{:S(2)}, u32[]{:S(2)}) collective-permute-start(f32[80]{0:T(128)S(1)} %slice.238), channel_id=1, source_target_pairs={{1,0},{2,1},{3,2},{4,3},{5,4},{6,5},{7,6},{8,7},{9,8},{10,9},{11,1... | collective-permute-start | bytes 968 | tf_op jit(solution)/shard_map/ppermute | solution.py:16
  53.0 182.5 %collective-permute-start.9 = (f32[]{:T(128)}, f32[]{:T(128)}, u32[]{:S(2)}, u32[]{:S(2)}) collective-permute-start(f32[]{:T(128)} %add.257), channel_id=1, source_target_pairs={{0,5},{1,6},{2,7},{3,8},{4,9},{5,10},{6,11},{7,12},{8,13},{9,14},{... | collective-permute-start | bytes 20 | tf_op jit(solution)/shard_map/ppermute | solution.py:16
  224.4 17.6 %collective-permute-start.10 = (f32[512]{0:T(512)S(1)}, f32[512]{0:T(512)S(1)}, u32[]{:S(2)}, u32[]{:S(2)}) collective-permute-start(f32[512]{0:T(512)S(1)} %bitcast.93), channel_id=1, source_target_pairs={{0,5},{1,6},{2,7},{3,8},{4,9},{5,10},{6,11},{7,12},{8,13},{9,14},{... | collective-permute-start | bytes 6152 | tf_op jit(solution)/shard_map/ppermute | solution.py:16
  226.9 18.4 %collective-permute-start.2 = (f32[512]{0:T(512)S(1)}, f32[512]{0:T(512)S(1)}, u32[]{:S(2)}, u32[]{:S(2)}) collective-permute-start(f32[512]{0:T(512)S(1)} %bitcast.94), channel_id=1, source_target_pairs={{0,1},{1,2},{2,3},{3,4},{4,5},{5,6},{6,7},{7,8},{8,9},{9,10},{10,1... | collective-permute-start | bytes 6152 | tf_op jit(solution)/shard_map/ppermute | solution.py:16
  230.6 19.1 %collective-permute-start.4 = (f32[512]{0:T(512)S(1)}, f32[512]{0:T(512)S(1)}, u32[]{:S(2)}, u32[]{:S(2)}) collective-permute-start(f32[512]{0:T(512)S(1)} %bitcast.95), channel_id=1, source_target_pairs={{0,2},{1,3},{2,4},{3,5},{4,6},{5,7},{6,8},{7,9},{8,10},{9,11},{10,... | collective-permute-start | bytes 6152 | tf_op jit(solution)/shard_map/ppermute | solution.py:16
  233.5 20.5 %collective-permute-start.6 = (f32[512]{0:T(512)S(1)}, f32[512]{0:T(512)S(1)}, u32[]{:S(2)}, u32[]{:S(2)}) collective-permute-start(f32[512]{0:T(512)S(1)} %bitcast.96), channel_id=1, source_target_pairs={{0,3},{1,4},{2,5},{3,6},{4,7},{5,8},{6,9},{7,10},{8,11},{9,12},{10... | collective-permute-start | bytes 6152 | tf_op jit(solution)/shard_map/ppermute | solution.py:16
  235.5 21.1 %collective-permute-start.8 = (f32[512]{0:T(512)S(1)}, f32[512]{0:T(512)S(1)}, u32[]{:S(2)}, u32[]{:S(2)}) collective-permute-start(f32[512]{0:T(512)S(1)} %bitcast.97), channel_id=1, source_target_pairs={{0,4},{1,5},{2,6},{3,7},{4,8},{5,9},{6,10},{7,11},{8,12},{9,13},{1... | collective-permute-start | bytes 6152 | tf_op jit(solution)/shard_map/ppermute | solution.py:16
  242.1 17.9 %collective-permute-start.11 = (f32[]{:T(128)}, f32[]{:T(128)}, u32[]{:S(2)}, u32[]{:S(2)}) collective-permute-start(f32[]{:T(128)} %add.258), channel_id=1, source_target_pairs={{1,0},{2,1},{3,2},{4,3},{5,4},{6,5},{7,6},{8,7},{9,8},{10,9},{11,1... | collective-permute-start | bytes 20 | tf_op jit(solution)/shard_map/ppermute | solution.py:16
  245.3 16.8 %collective-permute-start.13 = (f32[]{:T(128)}, f32[]{:T(128)}, u32[]{:S(2)}, u32[]{:S(2)}) collective-permute-start(f32[]{:T(128)} %add.258), channel_id=1, source_target_pairs={{2,0},{3,1},{4,2},{5,3},{6,4},{7,5},{8,6},{9,7},{10,8},{11,9},{12,... | collective-permute-start | bytes 20 | tf_op jit(solution)/shard_map/ppermute | solution.py:16
  249.7 14.4 %collective-permute-start.15 = (f32[]{:T(128)}, f32[]{:T(128)}, u32[]{:S(2)}, u32[]{:S(2)}) collective-permute-start(f32[]{:T(128)} %add.258), channel_id=1, source_target_pairs={{3,0},{4,1},{5,2},{6,3},{7,4},{8,5},{9,6},{10,7},{11,8},{12,9},{13... | collective-permute-start | bytes 20 | tf_op jit(solution)/shard_map/ppermute | solution.py:16
  254.0 12.0 %collective-permute-start.17 = (f32[]{:T(128)}, f32[]{:T(128)}, u32[]{:S(2)}, u32[]{:S(2)}) collective-permute-start(f32[]{:T(128)} %add.258), channel_id=1, source_target_pairs={{4,0},{5,1},{6,2},{7,3},{8,4},{9,5},{10,6},{11,7},{12,8},{13,9},{1... | collective-permute-start | bytes 20 | tf_op jit(solution)/shard_map/ppermute | solution.py:16
  256.6 11.3 %collective-permute-start.19 = (f32[]{:T(128)}, f32[]{:T(128)}, u32[]{:S(2)}, u32[]{:S(2)}) collective-permute-start(f32[]{:T(128)} %add.258), channel_id=1, source_target_pairs={{5,0},{6,1},{7,2},{8,3},{9,4},{10,5},{11,6},{12,7},{13,8},{14,9},{... | collective-permute-start | bytes 20 | tf_op jit(solution)/shard_map/ppermute | solution.py:16
  260.0 13.0 %collective-permute-start.12 = (f32[512]{0:T(512)S(1)}, f32[512]{0:T(512)S(1)}, u32[]{:S(2)}, u32[]{:S(2)}) collective-permute-start(f32[512]{0:T(512)S(1)} %bitcast.98), channel_id=1, source_target_pairs={{1,0},{2,1},{3,2},{4,3},{5,4},{6,5},{7,6},{8,7},{9,8},{10,9},{11,1... | collective-permute-start | bytes 6152 | tf_op jit(solution)/shard_map/ppermute | solution.py:16
  262.1 10.9 %collective-permute-start.14 = (f32[512]{0:T(512)S(1)}, f32[512]{0:T(512)S(1)}, u32[]{:S(2)}, u32[]{:S(2)}) collective-permute-start(f32[512]{0:T(512)S(1)} %bitcast.99), channel_id=1, source_target_pairs={{2,0},{3,1},{4,2},{5,3},{6,4},{7,5},{8,6},{9,7},{10,8},{11,9},{12,... | collective-permute-start | bytes 6152 | tf_op jit(solution)/shard_map/ppermute | solution.py:16
  264.1 9.0 %collective-permute-start.16 = (f32[512]{0:T(512)S(1)}, f32[512]{0:T(512)S(1)}, u32[]{:S(2)}, u32[]{:S(2)}) collective-permute-start(f32[512]{0:T(512)S(1)} %bitcast.100), channel_id=1, source_target_pairs={{3,0},{4,1},{5,2},{6,3},{7,4},{8,5},{9,6},{10,7},{11,8},{12,9},{13... | collective-permute-start | bytes 6152 | tf_op jit(solution)/shard_map/ppermute | solution.py:16
  266.0 7.0 %collective-permute-start.18 = (f32[512]{0:T(512)S(1)}, f32[512]{0:T(512)S(1)}, u32[]{:S(2)}, u32[]{:S(2)}) collective-permute-start(f32[512]{0:T(512)S(1)} %bitcast.101), channel_id=1, source_target_pairs={{4,0},{5,1},{6,2},{7,3},{8,4},{9,5},{10,6},{11,7},{12,8},{13,9},{1... | collective-permute-start | bytes 6152 | tf_op jit(solution)/shard_map/ppermute | solution.py:16
  267.9 8.1 %collective-permute-start.20 = (f32[512]{0:T(512)S(1)}, f32[512]{0:T(512)S(1)}, u32[]{:S(2)}, u32[]{:S(2)}) collective-permute-start(f32[512]{0:T(512)S(1)} %bitcast.102), channel_id=1, source_target_pairs={{5,0},{6,1},{7,2},{8,3},{9,4},{10,5},{11,6},{12,7},{13,8},{14,9},{... | collective-permute-start | bytes 6152 | tf_op jit(solution)/shard_map/ppermute | solution.py:16
  (6 other events, 82.8 us)
where the time goes:
time: 281 us; the launch traced here: 278 us
  local copies, waits for them, and re-layouts  93.8 us (33%)
  starting transfers between devices  71.6 us (25%)
  other arithmetic  55.2 us (20%)
  matrix products  31.6 us (11%)
  waiting for transfers between devices  13.2 us (5%)
  between operations  12.2 us (4%)
    slice x16, local copies, waits for them, and re-layouts, strided(): lax.slice_in_dim(inputs, offset, offset + stride * (length - 1) + 1, stri...  82.3 us
    ppermute x21, starting transfers between devices, from_behind(): lax.ppermute(value, axis, [(source, source + steps) for source in range(i...  60.2 us
    convert_element_type x7, other arithmetic, norm_gelu(): jax.nn.gelu(centred / jnp.sqrt(spread + 1e-05), approximate=False)  46 us
    dot_general x16, matrix products, strided(): jnp.dot(shifted, weight[offset], preferred_element_type=jnp.float32)  23.4 us
    all_to_all x1, waiting for transfers between devices, per_device(): lax.all_to_all(send_rows, 'dp', split_axis=0, concat_axis=0, tiled=True)  7.19 us
    dot_general x1, matrix products, first_layer(): jnp.dot(patches, first_weight, precision=lax.Precision.HIGHEST, preferred...  7.02 us
    all_to_all x1, starting transfers between devices, per_device(): lax.all_to_all(send_rows, 'dp', split_axis=0, concat_axis=0, tiled=True)  6.09 us
    ppermute x21, waiting for transfers between devices, from_behind(): lax.ppermute(value, axis, [(source, source + steps) for source in range(i...  6.03 us
  transfers between devices with their start and end apart: 23, of which 3 were waited for; matrix products, arithmetic and copies ran while one was open for 63% of the time, Pallas kernels for 0%

commit v1 on v0

v1 whole, which is shorter than its diff:
```python
import functools

import jax
import jax.numpy as jnp
from jax import lax
from jax.experimental import pallas as pl
from jax.experimental.pallas import tpu as pltpu
from jax.sharding import PartitionSpec as P

BLOCK = 320
WIDE = 384
MAXLEN = 256
EPS = 1e-05
HALF_ROOT = 0.7071067811865476
HIGHEST = lax.Precision.HIGHEST
F32 = jnp.float32
BF16 = jnp.bfloat16


def iota(shape, dim):
    return lax.broadcasted_iota(jnp.int32, shape, dim).astype(F32)


def to_column(row):
    size = row.shape[1]
    same = iota((size, size), 0) == iota((size, size), 1)
    return jnp.sum(jnp.where(same, row, 0.0), axis=1, keepdims=True)


def starts_column(length_row):
    size = length_row.shape[1]
    earlier = iota((size, size), 1) < iota((size, size), 0)
    return jnp.sum(jnp.where(earlier, length_row, 0.0), axis=1, keepdims=True)


def norm_gelu(values):
    average = jnp.mean(values, axis=-1, keepdims=True)
    centred = values - average
    spread = jnp.mean(centred * centred, axis=-1, keepdims=True)
    scaled = centred * (lax.rsqrt(spread + EPS) * HALF_ROOT)
    half = scaled * HALF_ROOT
    return half + half * lax.erf(scaled)


def route_kernel(n, cap, stride, wave_ref, slot_ref, out_ref, wide, send, recv, send_sem, recv_sem):
    me = lax.axis_index("dp")

    def greet(k, carry):
        pl.semaphore_signal(
            pltpu.get_barrier_semaphore(), inc=1, device_id={"dp": lax.rem(me + k, n)}
        )
        return carry

    lax.fori_loop(1, n, greet, 0)
    rows = wave_ref.shape[0]
    slot_row = slot_ref[...].astype(F32)
    slot_col = to_column(slot_row)
    target_row = jnp.floor(slot_row / rows)
    target_col = jnp.floor(slot_col / rows)
    earlier = (iota((rows, rows), 0) < iota((rows, rows), 1)) & (target_col == target_row)
    rank_row = jnp.sum(jnp.where(earlier, 1.0, 0.0), axis=0, keepdims=True)
    dest_row = target_row * stride + rank_row
    ahead_row = jnp.where(target_row * rows == slot_row, (target_row - 1.0) * stride + cap, -1.0)
    place = iota((n * stride, rows), 0)
    pick = jnp.where((place == dest_row) | (place == ahead_row), 1.0, 0.0)
    wide[:, :BLOCK] = wave_ref[...]
    wide[:, BLOCK:] = jnp.where(iota((rows, WIDE - BLOCK), 1) == 0.0, slot_col + 1.0, 0.0)
    send[...] = jnp.dot(pick, wide[...], precision=HIGHEST, preferred_element_type=F32)
    mine = pl.ds(pl.multiple_of(me * stride, stride), stride)
    recv[mine, :] = send[mine, :]
    pl.semaphore_wait(pltpu.get_barrier_semaphore(), n - 1)

    def copy_to(k):
        to = lax.rem(me + k, n)
        return pltpu.make_async_remote_copy(
            src_ref=send.at[pl.ds(pl.multiple_of(to * stride, stride), stride)],
            dst_ref=recv.at[mine],
            send_sem=send_sem.at[to],
            recv_sem=recv_sem.at[me],
            device_id={"dp": to},
        )

    def copy_from(k):
        source = lax.rem(me + n - k, n)
        return pltpu.make_async_remote_copy(
            src_ref=send.at[mine],
            dst_ref=recv.at[pl.ds(pl.multiple_of(source * stride, stride), stride)],
            send_sem=send_sem.at[me],
            recv_sem=recv_sem.at[source],
            device_id={"dp": source},
        )

    def begin(k, carry):
        copy_to(k).start()
        return carry

    def finish(k, carry):
        copy_from(k).wait_recv()
        copy_to(k).wait_send()
        return carry

    lax.fori_loop(1, n, begin, 0)
    lax.fori_loop(1, n, finish, 0)
    out_ref[...] = recv[...]


def conv_kernel(
    recv_ref, length_ref, trim_ref, first_ref, mid_ref, tail_ref, out_ref,
    xs, e1, o1, e2, o2, e3, o3, e4, o4, e5, o5, e6, o6, h1, h2, h3, acc,
):
    me = lax.axis_index("dp").astype(F32)
    rows = out_ref.shape[0]
    length_row = length_ref[...].astype(F32)
    trim_col = to_column(trim_ref[...].astype(F32))
    start = starts_column(length_row)
    end = start + to_column(length_row)
    count = length_row.shape[1]
    frame = iota((count, 128), 1) + me * rows
    limit = jnp.sum(
        jnp.where((start <= frame) & (frame < end), BLOCK * (end - frame) - trim_col, 0.0),
        axis=0,
        keepdims=True,
    )
    got = recv_ref.shape[0]
    slot = recv_ref[:, BLOCK : BLOCK + 1] - 1.0 - me * rows
    lane = iota((got, 128), 1)
    spread = jnp.where((slot == lane) & (lane <= rows), 1.0, 0.0)
    wave = jnp.transpose(recv_ref[...])[:BLOCK]
    stream = jnp.dot(wave, spread, precision=HIGHEST, preferred_element_type=F32)
    signal = jnp.where(iota((BLOCK, 128), 0) < limit, stream, 0.0)
    part1 = signal.astype(BF16).astype(F32)
    rest = signal - part1
    part2 = rest.astype(BF16).astype(F32)
    part3 = rest - part2
    for index, part in enumerate((part1, part2, part3)):
        xs[index, :BLOCK, :] = part
        xs[index, BLOCK : BLOCK + 8, :] = pltpu.roll(part[:8], 127, 1)
        xs[index, BLOCK + 8 :, :] = jnp.zeros((8, 128), F32)

    first = first_ref[...]
    weight1 = first.astype(BF16).astype(F32)
    left = first - weight1
    weight2 = left.astype(BF16).astype(F32)
    weight3 = left - weight2
    kernel1 = jnp.concatenate([weight1, weight2, weight1, weight2, weight3, weight1], axis=0).astype(BF16)

    def patches(phase):
        a, b, c = [xs[index, pl.ds(5 * phase, 16), :] for index in range(3)]
        return jnp.concatenate([a, a, b, b, a, c], axis=0)

    def first_dot(block):
        return lax.dot_general(
            block.astype(BF16), kernel1, (((0,), (0,)), ((), ())), preferred_element_type=F32
        )

    def gather_halo(phase, total):
        return jnp.where(
            lax.broadcasted_iota(jnp.int32, (96, 128), 1) == phase, patches(phase)[:, rows : rows + 1], total
        )

    halo = lax.fori_loop(0, 16, gather_halo, jnp.zeros((96, 128), F32))
    h1[:16, :] = norm_gelu(first_dot(halo[:, :16])).astype(BF16).astype(F32)
    h1[16:, :] = jnp.zeros_like(h1[16:, :])

    def first_step(step, carry):
        where = pl.ds(pl.multiple_of(step * rows, rows), rows)
        for parity, dest in ((0, e1), (1, o1)):
            acc[parity * rows : (parity + 1) * rows, :] = first_dot(patches(2 * step + parity)[:, :rows])
        for parity, dest in ((0, e1), (1, o1)):
            for r in range(0, rows, 16):
                block = acc[parity * rows + r : parity * rows + r + 16, :]
                dest[pl.ds(pl.multiple_of(step * rows + r, 16), 16), :] = norm_gelu(block).astype(BF16)
        return carry

    lax.fori_loop(0, 32, first_step, 0)

    def wrap(even, halo_ref, phases):
        rolled = pltpu.roll(even[:rows, :].astype(F32), rows - 1, 0)
        shifted = jnp.where(iota(rolled.shape, 0) == rows - 1, halo_ref[0:1, :], rolled)
        even[pl.ds(phases // 2 * rows, rows), :] = shifted.astype(BF16)

    def layer(even, odd, taps, dest_even, dest_odd, phases):
        chunk = min(phases, 4)
        size = chunk * rows

        def step(index, carry):
            base = pl.multiple_of(index * size, size)
            inputs = [even[pl.ds(base, size), :], odd[pl.ds(base, size), :]]
            if len(taps) == 3:
                inputs.append(even[pl.ds(pl.multiple_of(base + rows, rows), size), :])
            total = None
            for value, tap in zip(inputs, taps):
                term = jnp.dot(value, tap[...], preferred_element_type=F32)
                total = term if total is None else total + term
            acc[:size, :] = total
            for p in range(chunk):
                dest = dest_even if p % 2 == 0 else dest_odd
                for r in range(0, rows, 16):
                    block = acc[p * rows + r : p * rows + r + 16, :]
                    at = index * (size // 2) + p // 2 * rows + r
                    if chunk == 1:
                        at = r
                    dest[pl.ds(pl.multiple_of(at, 16), 16), :] = norm_gelu(block).astype(BF16)
            return carry

        if phases == chunk:
            step(0, 0)
        else:
            lax.fori_loop(0, phases // chunk, step, 0)

    def halo_layer(source, dest, taps):
        total = None
        for offset, tap in enumerate(taps):
            choose = jnp.where(iota((16, 24), 1) == 2.0 * iota((16, 24), 0) + offset, 1.0, 0.0)
            value = jnp.dot(
                choose.astype(BF16), source[...].astype(BF16), preferred_element_type=F32
            ).astype(BF16)
            term = jnp.dot(value, tap[...], preferred_element_type=F32)
            total = term if total is None else total + term
        dest[:8, :] = norm_gelu(total[:8]).astype(BF16).astype(F32)
        dest[8:, :] = jnp.zeros_like(dest[8:, :])

    mids = [[mid_ref.at[i, t] for t in range(3)] for i in range(4)]
    tails = [[tail_ref.at[i, t] for t in range(2)] for i in range(2)]
    wrap(e1, h1, 64)
    halo_layer(h1, h2, mids[0])
    layer(e1, o1, mids[0], e2, o2, 32)
    wrap(e2, h2, 32)
    halo_layer(h2, h3, mids[1])
    layer(e2, o2, mids[1], e3, o3, 16)
    wrap(e3, h3, 16)
    halo_layer(h3, h1, mids[2])
    layer(e3, o3, mids[2], e4, o4, 8)
    wrap(e4, h1, 8)
    layer(e4, o4, mids[3], e5, o5, 4)
    layer(e5, o5, tails[0], e6, o6, 2)
    layer(e6, o6, tails[1], out_ref, out_ref, 1)


def mean_kernel(n, reach, feature_ref, length_ref, out_ref, send, recv, send_sem, recv_sem):
    me = lax.axis_index("dp")
    rows, channels = feature_ref.shape
    pieces = channels // 128
    recv[...] = jnp.zeros_like(recv)
    barrier = pltpu.get_barrier_semaphore()
    links = [(k, k - 1) for k in range(1, reach + 1)] + [(-k, reach + k - 1) for k in range(1, reach + 1)]

    def inside(k):
        return (me + k < n) & (me + k >= 0)

    for k, _ in links:
        @pl.when(inside(k))
        def _():
            pl.semaphore_signal(barrier, inc=1, device_id={"dp": me + k})

    base = me.astype(F32) * rows
    length_row = length_ref[...].astype(F32)
    start = starts_column(length_row)
    end = start + to_column(length_row)
    frame = iota((length_row.shape[1], rows), 1) + base
    member = (start <= frame) & (frame < end)
    start_row = jnp.sum(jnp.where(member, start, 0.0), axis=0, keepdims=True)
    end_row = jnp.sum(jnp.where(member, end, 0.0), axis=0, keepdims=True)
    start_col = to_column(start_row)
    end_col = to_column(end_row)
    features = feature_ref[...]
    line = iota((16, rows), 1) + base
    last = line >= start_row[:, rows - 1 : rows]
    initial = line < end_row[:, 0:1]
    pick = jnp.where(iota((16, rows), 0) == 0.0, jnp.where(last, 1.0, 0.0), jnp.where(initial, 1.0, 0.0))
    edges = jnp.dot(pick.astype(BF16), features, preferred_element_type=F32)
    send[...] = jnp.zeros_like(send)
    for index in range(2):
        for piece in range(pieces):
            send[index, piece : piece + 1, :] = edges[index : index + 1, piece * 128 : piece * 128 + 128]

    def copy(k, slot):
        return pltpu.make_async_remote_copy(
            src_ref=send.at[0 if k > 0 else 1],
            dst_ref=recv.at[slot],
            send_sem=send_sem.at[slot],
            recv_sem=recv_sem.at[slot],
            device_id={"dp": me + k},
        )

    for place in range(n):
        if place < reach or place >= n - reach:
            @pl.when(me == place)
            def _():
                pl.semaphore_wait(barrier, min(place, reach) + min(n - 1 - place, reach))

    @pl.when((me >= reach) & (me < n - reach))
    def _():
        pl.semaphore_wait(barrier, 2 * reach)

    for k, slot in links:
        @pl.when(inside(k))
        def _():
            copy(k, slot).start()
    local = iota((rows, rows), 1) + base
    within = jnp.where((start_col <= local) & (local < end_col), 1.0, 0.0).astype(BF16)
    totals = jnp.dot(within, features, preferred_element_type=F32)
    for k, slot in links:
        @pl.when(inside(-k))
        def _():
            copy(-k, slot).wait_recv()

        @pl.when(inside(k))
        def _():
            copy(k, slot).wait_send()
    for k, slot in links:
        row = jnp.concatenate([recv[slot, piece : piece + 1, :] for piece in range(pieces)], axis=1)
        if k > 0:
            reached = start_col <= base - (k - 1) * rows - 1.0
        else:
            reached = end_col > base - k * rows
        totals = totals + jnp.where(reached, row, 0.0)
    out_ref[...] = (features.astype(F32) - totals / (end_col - start_col)).astype(BF16)


def per_device(wave, row_slot, frame_lengths, sample_trim, first_weight, mid_weight, tail_weight):
    rows = wave.shape[0]
    channels = first_weight.shape[1]
    n = lax.axis_size("dp")
    cap = rows // n + 2
    stride = (cap + 1 + 7) // 8 * 8
    reach = min((MAXLEN + rows - 2) // rows, n - 1)
    vmem = pl.BlockSpec(memory_space=pltpu.VMEM)
    lengths = frame_lengths.reshape(1, -1)
    received = pl.pallas_call(
        functools.partial(route_kernel, n, cap, stride),
        out_shape=jax.ShapeDtypeStruct((n * stride, WIDE), F32),
        in_specs=[vmem] * 2,
        out_specs=vmem,
        scratch_shapes=[
            pltpu.VMEM((rows, WIDE), F32),
            pltpu.VMEM((n * stride, WIDE), F32),
            pltpu.VMEM((n * stride, WIDE), F32),
            pltpu.SemaphoreType.DMA((n,)),
            pltpu.SemaphoreType.DMA((n,)),
        ],
        compiler_params=pltpu.CompilerParams(collective_id=0, has_side_effects=True),
        name="route",
    )(wave, row_slot.reshape(1, -1))
    first = jnp.pad(first_weight, ((0, 6), (0, 0)))

    def slab(phases):
        return pltpu.VMEM((phases * rows, channels), BF16)

    features = pl.pallas_call(
        conv_kernel,
        out_shape=jax.ShapeDtypeStruct((rows, channels), BF16),
        in_specs=[vmem] * 6,
        out_specs=vmem,
        scratch_shapes=[
            pltpu.VMEM((3, BLOCK + 16, 128), F32),
            slab(33), slab(32), slab(17), slab(16), slab(9), slab(8), slab(5), slab(4),
            slab(2), slab(2), slab(1), slab(1),
            pltpu.VMEM((24, channels), F32),
            pltpu.VMEM((24, channels), F32),
            pltpu.VMEM((24, channels), F32),
            pltpu.VMEM((4 * rows, channels), F32),
        ],
        compiler_params=pltpu.CompilerParams(vmem_limit_bytes=48 * 1024 * 1024),
        name="convs",
    )(received, lengths, sample_trim.reshape(1, -1), first, mid_weight, tail_weight)
    return pl.pallas_call(
        functools.partial(mean_kernel, n, reach),
        out_shape=jax.ShapeDtypeStruct((rows, channels), BF16),
        in_specs=[vmem] * 2,
        out_specs=vmem,
        scratch_shapes=[
            pltpu.VMEM((2, 8, 128), F32),
            pltpu.VMEM((2 * reach, 8, 128), F32),
            pltpu.SemaphoreType.DMA((2 * reach,)),
            pltpu.SemaphoreType.DMA((2 * reach,)),
        ],
        compiler_params=pltpu.CompilerParams(collective_id=1, has_side_effects=True),
        name="means",
    )(features, lengths)


def solution(mesh):
    placed = (
        P(("groups", "dp"), None),
        P(("groups", "dp")),
        P("groups"),
        P("groups"),
        P(),
        P(),
        P(),
    )
    return jax.shard_map(
        per_device, mesh=mesh, in_specs=placed, out_specs=P(("groups", "dp"), None), check_vma=False
    )
```

time: 281 us -> 59.1 us (0.21)
  the two profiles are of different devices: /device:TPU:11 before, /device:TPU:0 now
where the time goes in v1:
time: 59.1 us; the launch traced here: 58.7 us
  Pallas kernels  52 us (88%)
  local copies, waits for them, and re-layouts  6.68 us (11%)
    pallas_call x1, Pallas kernels, per_device(): pl.pallas_call(conv_kernel, out_shape=jax.ShapeDtypeStruct((rows, channel...  33 us
    pallas_call x1, Pallas kernels, per_device(): pl.pallas_call(functools.partial(route_kernel, n, cap, stride), out_shape...  11.6 us
    pallas_call x1, Pallas kernels, per_device(): pl.pallas_call(functools.partial(mean_kernel, n, reach), out_shape=jax.Sh...  7.35 us
    unnamed x11, local copies, waits for them, and re-layouts  5.92 us

profile of v1, /device:TPU:0, one launch (start us, length us, event | category | flops | bytes accessed | tf_op | source)
XLA Modules:
  0.0 58.7 jit_solution(6268976378572194000)
XLA Ops:
  0.0 0.8 %pad.4.first_ref = f32[16,512]{1,0:T(8,128)S(1)} pad(f32[10,512]{1,0:T(8,128)} %param.11, f32[]{:T(128)} %constant.2.clone.1), padding=0_6x0_0 | pad | bytes 53252 | tf_op jit(solution)/shard_map/jit(_pad)/pad | solution.py:345
  0.8 11.6 %route.1.recv_ref = f32[128,384]{1,0:T(8,128)} custom-call(f32[64,320]{1,0:T(8,128)} %wave_ref.1, s32[1,64]{1,0:T(1,128)} %bitcast.6), custom_call_target="tpu_custom_call" | custom-call | tf_op jit(solution)/shard_map/route/pallas_call | solution.py:330
  12.4 0.0 copy-start
  12.4 1.6 %copy-done = bf16[2,2,512,512]{3,2,1,0:T(8,128)(2,1)S(1)} copy-done((bf16[2,2,512,512]{3,2,1,0:T(8,128)(2,1)S(1)}, bf16[2,2,512,512]{3,2,1,0:T(8,128)(2,1)}, u32[]{:S(2)}) %copy-start) | copy-done | bytes 2097176
  14.0 0.0 copy-start.1
  14.0 0.9 %copy-done.1 = f32[128,384]{1,0:T(8,128)S(1)} copy-done((f32[128,384]{1,0:T(8,128)S(1)}, f32[128,384]{1,0:T(8,128)}, u32[]{:S(2)}) %copy-start.1) | copy-done | bytes 196632
  14.9 0.0 copy-start.3
  14.9 0.7 %copy-done.3 = s32[64]{0:T(128)S(1)} copy-done((s32[64]{0:T(128)S(1)}, s32[64]{0:T(128)}, u32[]{:S(2)}) %copy-start.3) | copy-done | bytes 280
  15.6 0.0 copy-start.4
  15.6 0.7 %copy-done.4 = s32[64]{0:T(128)S(1)} copy-done((s32[64]{0:T(128)S(1)}, s32[64]{0:T(128)}, u32[]{:S(2)}) %copy-start.4) | copy-done | bytes 280
  16.2 33.0 %convs.1.feature_ref = bf16[64,512]{1,0:T(8,128)(2,1)S(1)} custom-call(f32[128,384]{1,0:T(8,128)S(1)} %copy-done.1, s32[1,64]{1,0:T(1,128)S(1)} %bitcast.4, s32[1,64]{1,0:T(1,128)S(1)} %bitcast.5, f32[16,512]{1,0:T(8,128)S(1)} %pad.4.first_ref, bf16[4,3,512,512]{3,2,1,0:T(8,128)(2,1)} %mid_ref.1, bf16[2,2,512,512]{3,2,1,0:T(8,128)(2,1)S(1)} %copy-done), custom_call_target="tpu_custom_call" | custom-call | tf_op jit(solution)/shard_map/convs/pallas_call | solution.py:350
  49.2 0.0 copy-start.2
  49.3 0.6 %copy-done.2 = bf16[64,512]{1,0:T(8,128)(2,1)} copy-done((bf16[64,512]{1,0:T(8,128)(2,1)}, bf16[64,512]{1,0:T(8,128)(2,1)S(1)}, u32[]{:S(2)}) %copy-start.2) | copy-done | bytes 65560
  49.9 7.3 %means.1 = bf16[64,512]{1,0:T(8,128)(2,1)} custom-call(bf16[64,512]{1,0:T(8,128)(2,1)} %copy-done.2, s32[1,64]{1,0:T(1,128)} %bitcast.3), custom_call_target="tpu_custom_call" | custom-call | tf_op jit(solution)/shard_map/means/pallas_call | solution.py:367
  57.2 1.5 %copy.9 = bf16[64,512]{1,0:T(8,128)(2,1)} copy(bf16[64,512]{1,0:T(8,128)(2,1)} %means.1) | data formatting | bytes 131072
Async XLA Ops:
  12.4 1.6 %copy-start = (bf16[2,2,512,512]{3,2,1,0:T(8,128)(2,1)S(1)}, bf16[2,2,512,512]{3,2,1,0:T(8,128)(2,1)}, u32[]{:S(2)}) copy-start(bf16[2,2,512,512]{3,2,1,0:T(8,128)(2,1)} %tail_ref.1) | copy-start | bytes 6291460
  14.0 0.9 %copy-start.1 = (f32[128,384]{1,0:T(8,128)S(1)}, f32[128,384]{1,0:T(8,128)}, u32[]{:S(2)}) copy-start(f32[128,384]{1,0:T(8,128)} %route.1.recv_ref) | copy-start | bytes 589828
  14.9 0.7 %copy-start.3 = (s32[64]{0:T(128)S(1)}, s32[64]{0:T(128)}, u32[]{:S(2)}) copy-start(s32[64]{0:T(128)} %param.9) | copy-start | bytes 772
  15.6 0.7 %copy-start.4 = (s32[64]{0:T(128)S(1)}, s32[64]{0:T(128)}, u32[]{:S(2)}) copy-start(s32[64]{0:T(128)} %param.10) | copy-start | bytes 772
  49.2 0.6 %copy-start.2 = (bf16[64,512]{1,0:T(8,128)(2,1)}, bf16[64,512]{1,0:T(8,128)(2,1)S(1)}, u32[]{:S(2)}) copy-start(bf16[64,512]{1,0:T(8,128)(2,1)S(1)} %convs.1.feature_ref) | copy-start | bytes 196612

commit v2 on v1

--- a/solution.py
+++ b/solution.py
@@ -42,7 +42,7 @@
     return half + half * lax.erf(scaled)
 
 
-def route_kernel(n, cap, stride, wave_ref, slot_ref, out_ref, wide, send, recv, send_sem, recv_sem):
+def route(n, cap, stride, wave_ref, slot_ref, wide, send, recv, send_sem, recv_sem):
     me = lax.axis_index("dp")
 
     def greet(k, carry):
@@ -101,12 +101,11 @@
 
     lax.fori_loop(1, n, begin, 0)
     lax.fori_loop(1, n, finish, 0)
-    out_ref[...] = recv[...]
-
-
-def conv_kernel(
-    recv_ref, length_ref, trim_ref, first_ref, mid_ref, tail_ref, out_ref,
-    xs, e1, o1, e2, o2, e3, o3, e4, o4, e5, o5, e6, o6, h1, h2, h3, acc,
+
+
+def convs(
+    ready, recv_ref, length_ref, trim_ref, first_ref, mid_ref, tail_ref, out_ref,
+    xs, pad, e1, o1, e2, o2, e3, o3, e4, o4, e5, o5, e6, o6, h1, h2, h3, acc,
 ):
     me = lax.axis_index("dp").astype(F32)
     rows = out_ref.shape[0]
@@ -137,7 +136,9 @@
         xs[index, BLOCK : BLOCK + 8, :] = pltpu.roll(part[:8], 127, 1)
         xs[index, BLOCK + 8 :, :] = jnp.zeros((8, 128), F32)
 
-    first = first_ref[...]
+    pad[...] = jnp.zeros_like(pad)
+    pad[: first_ref.shape[0], :] = first_ref[...]
+    first = pad[...]
     weight1 = first.astype(BF16).astype(F32)
     left = first - weight1
     weight2 = left.astype(BF16).astype(F32)
@@ -222,36 +223,34 @@
 
     mids = [[mid_ref.at[i, t] for t in range(3)] for i in range(4)]
     tails = [[tail_ref.at[i, t] for t in range(2)] for i in range(2)]
+    ready(0)
     wrap(e1, h1, 64)
     halo_layer(h1, h2, mids[0])
     layer(e1, o1, mids[0], e2, o2, 32)
+    ready(1)
     wrap(e2, h2, 32)
     halo_layer(h2, h3, mids[1])
     layer(e2, o2, mids[1], e3, o3, 16)
+    ready(2)
     wrap(e3, h3, 16)
     halo_layer(h3, h1, mids[2])
     layer(e3, o3, mids[2], e4, o4, 8)
+    ready(3)
     wrap(e4, h1, 8)
     layer(e4, o4, mids[3], e5, o5, 4)
+    ready(4)
     layer(e5, o5, tails[0], e6, o6, 2)
     layer(e6, o6, tails[1], out_ref, out_ref, 1)
 
 
-def mean_kernel(n, reach, feature_ref, length_ref, out_ref, send, recv, send_sem, recv_sem):
+def means(n, reach, feature_ref, length_ref, out_ref, send, recv, send_sem, recv_sem):
     me = lax.axis_index("dp")
     rows, channels = feature_ref.shape
     pieces = channels // 128
-    recv[...] = jnp.zeros_like(recv)
-    barrier = pltpu.get_barrier_semaphore()
     links = [(k, k - 1) for k in range(1, reach + 1)] + [(-k, reach + k - 1) for k in range(1, reach + 1)]
 
     def inside(k):
         return (me + k < n) & (me + k >= 0)
-
-    for k, _ in links:
-        @pl.when(inside(k))
-        def _():
-            pl.semaphore_signal(barrier, inc=1, device_id={"dp": me + k})
 
     base = me.astype(F32) * rows
     length_row = length_ref[...].astype(F32)
@@ -283,16 +282,6 @@
             device_id={"dp": me + k},
         )
 
-    for place in range(n):
-        if place < reach or place >= n - reach:
-            @pl.when(me == place)
-            def _():
-                pl.semaphore_wait(barrier, min(place, reach) + min(n - 1 - place, reach))
-
-    @pl.when((me >= reach) & (me < n - reach))
-    def _():
-        pl.semaphore_wait(barrier, 2 * reach)
-
     for k, slot in links:
         @pl.when(inside(k))
         def _():
@@ -318,6 +307,25 @@
     out_ref[...] = (features.astype(F32) - totals / (end_col - start_col)).astype(BF16)
 
 
+def frontend_kernel(
+    n, cap, stride, reach,
+    wave_ref, slot_ref, length_ref, trim_ref, first_ref, mid_hbm, tail_hbm, out_ref,
+    wide, send, recv, send_sem, recv_sem,
+    mid, tail, weight_sem, features, edges, far, edge_send_sem, edge_recv_sem, *work,
+):
+    loads = [pltpu.make_async_copy(mid_hbm.at[i], mid.at[i], weight_sem.at[i]) for i in range(4)]
+    loads.append(pltpu.make_async_copy(tail_hbm, tail, weight_sem.at[4]))
+    for load in loads:
+        load.start()
+    far[...] = jnp.zeros_like(far)
+    route(n, cap, stride, wave_ref, slot_ref, wide, send, recv, send_sem, recv_sem)
+    convs(
+        lambda i: loads[i].wait(),
+        recv, length_ref, trim_ref, first_ref, mid, tail, features, *work,
+    )
+    means(n, reach, features, length_ref, out_ref, edges, far, edge_send_sem, edge_recv_sem)
+
+
 def per_device(wave, row_slot, frame_lengths, sample_trim, first_weight, mid_weight, tail_weight):
     rows = wave.shape[0]
     channels = first_weight.shape[1]
@@ -326,11 +334,15 @@
     stride = (cap + 1 + 7) // 8 * 8
     reach = min((MAXLEN + rows - 2) // rows, n - 1)
     vmem = pl.BlockSpec(memory_space=pltpu.VMEM)
-    lengths = frame_lengths.reshape(1, -1)
-    received = pl.pallas_call(
-        functools.partial(route_kernel, n, cap, stride),
-        out_shape=jax.ShapeDtypeStruct((n * stride, WIDE), F32),
-        in_specs=[vmem] * 2,
+    outside = pl.BlockSpec(memory_space=pl.ANY)
+
+    def slab(phases):
+        return pltpu.VMEM((phases * rows, channels), BF16)
+
+    return pl.pallas_call(
+        functools.partial(frontend_kernel, n, cap, stride, reach),
+        out_shape=jax.ShapeDtypeStruct((rows, channels), BF16),
+        in_specs=[vmem] * 5 + [outside] * 2,
         out_specs=vmem,
         scratch_shapes=[
             pltpu.VMEM((rows, WIDE), F32),
@@ -338,22 +350,16 @@
             pltpu.VMEM((n * stride, WIDE), F32),
             pltpu.SemaphoreType.DMA((n,)),
             pltpu.SemaphoreType.DMA((n,)),
-        ],
-        compiler_params=pltpu.CompilerParams(collective_id=0, has_side_effects=True),
-        name="route",
-    )(wave, row_slot.reshape(1, -1))
-    first = jnp.pad(first_weight, ((0, 6), (0, 0)))
-
-    def slab(phases):
-        return pltpu.VMEM((phases * rows, channels), BF16)
-
-    features = pl.pallas_call(
-        conv_kernel,
-        out_shape=jax.ShapeDtypeStruct((rows, channels), BF16),
-        in_specs=[vmem] * 6,
-        out_specs=vmem,
-        scratch_shapes=[
+            pltpu.VMEM(mid_weight.shape, BF16),
+            pltpu.VMEM(tail_weight.shape, BF16),
+            pltpu.SemaphoreType.DMA((5,)),
+            pltpu.VMEM((rows, channels), BF16),
+            pltpu.VMEM((2, 8, 128), F32),
+            pltpu.VMEM((2 * reach, 8, 128), F32),
+            pltpu.SemaphoreType.DMA((2 * reach,)),
+            pltpu.SemaphoreType.DMA((2 * reach,)),
             pltpu.VMEM((3, BLOCK + 16, 128), F32),
+            pltpu.VMEM((16, channels), F32),
             slab(33), slab(32), slab(17), slab(16), slab(9), slab(8), slab(5), slab(4),
             slab(2), slab(2), slab(1), slab(1),
             pltpu.VMEM((24, channels), F32),
@@ -361,23 +367,14 @@
             pltpu.VMEM((24, channels), F32),
             pltpu.VMEM((4 * rows, channels), F32),
         ],
-        compiler_params=pltpu.CompilerParams(vmem_limit_bytes=48 * 1024 * 1024),
-        name="convs",
-    )(received, lengths, sample_trim.reshape(1, -1), first, mid_weight, tail_weight)
-    return pl.pallas_call(
-        functools.partial(mean_kernel, n, reach),
-        out_shape=jax.ShapeDtypeStruct((rows, channels), BF16),
-        in_specs=[vmem] * 2,
-        out_specs=vmem,
-        scratch_shapes=[
-            pltpu.VMEM((2, 8, 128), F32),
-            pltpu.VMEM((2 * reach, 8, 128), F32),
-            pltpu.SemaphoreType.DMA((2 * reach,)),
-            pltpu.SemaphoreType.DMA((2 * reach,)),
-        ],
-        compiler_params=pltpu.CompilerParams(collective_id=1, has_side_effects=True),
-        name="means",
-    )(features, lengths)
+        compiler_params=pltpu.CompilerParams(
+            collective_id=0, has_side_effects=True, vmem_limit_bytes=48 * 1024 * 1024
+        ),
+        name="frontend",
+    )(
+        wave, row_slot.reshape(1, -1), frame_lengths.reshape(1, -1), sample_trim.reshape(1, -1),
+        first_weight, mid_weight, tail_weight,
+    )
 
 
 def solution(mesh):

time: 59.1 us -> 51.3 us (0.87)
  Pallas kernels: 52 us -> 45.1 us
  local copies, waits for them, and re-layouts: 6.68 us -> 5.84 us
    pallas_call x3 -> x1, Pallas kernels: 52 us -> 45.1 us  [per_device(): pl.pallas_call(functools.partial(frontend_kernel, n, cap, stride, reach),...]
    pad x1 -> x0, local copies, waits for them, and re-layouts: 0.76 us -> none  [per_device(): first = jnp.pad(first_weight, ((0, 6), (0, 0)))]
    unnamed x11 -> x13, local copies, waits for them, and re-layouts: 5.92 us -> 5.84 us
where the time goes in v2:
time: 51.3 us; the launch traced here: 51 us
  Pallas kernels  45.1 us (88%)
  local copies, waits for them, and re-layouts  5.84 us (11%)
    pallas_call x1, Pallas kernels, per_device(): pl.pallas_call(functools.partial(frontend_kernel, n, cap, stride, reach),...  45.1 us
    unnamed x13, local copies, waits for them, and re-layouts  5.84 us

profile of v2, /device:TPU:0, one launch (start us, length us, event | category | flops | bytes accessed | tf_op | source)
XLA Modules:
  0.0 51.0 jit_solution(13288024039916941655)
XLA Ops:
  0.0 0.0 copy-start
  0.0 1.6 %copy-done = bf16[2,2,512,512]{3,2,1,0:T(8,128)(2,1)S(1)} copy-done((bf16[2,2,512,512]{3,2,1,0:T(8,128)(2,1)S(1)}, bf16[2,2,512,512]{3,2,1,0:T(8,128)(2,1)}, u32[]{:S(2)}) %copy-start) | copy-done | bytes 2097176
  1.6 0.0 copy-start.1
  1.6 0.9 %copy-done.1 = f32[64,320]{1,0:T(8,128)S(1)} copy-done((f32[64,320]{1,0:T(8,128)S(1)}, f32[64,320]{1,0:T(8,128)}, u32[]{:S(2)}) %copy-start.1) | copy-done | bytes 81944
  2.5 0.0 copy-start.2
  2.5 0.8 %copy-done.2 = f32[10,512]{1,0:T(8,128)S(1)} copy-done((f32[10,512]{1,0:T(8,128)S(1)}, f32[10,512]{1,0:T(8,128)}, u32[]{:S(2)}) %copy-start.2) | copy-done | bytes 20504
  3.2 0.0 copy-start.3
  3.2 0.7 %copy-done.3 = s32[64]{0:T(128)S(1)} copy-done((s32[64]{0:T(128)S(1)}, s32[64]{0:T(128)}, u32[]{:S(2)}) %copy-start.3) | copy-done | bytes 280
  3.9 0.0 copy-start.4
  3.9 0.7 %copy-done.4 = s32[64]{0:T(128)S(1)} copy-done((s32[64]{0:T(128)S(1)}, s32[64]{0:T(128)}, u32[]{:S(2)}) %copy-start.4) | copy-done | bytes 280
  4.6 0.0 copy-start.5
  4.6 0.7 %copy-done.5 = s32[64]{0:T(128)S(1)} copy-done((s32[64]{0:T(128)S(1)}, s32[64]{0:T(128)}, u32[]{:S(2)}) %copy-start.5) | copy-done | bytes 280
  5.2 45.1 %frontend.1 = bf16[64,512]{1,0:T(8,128)(2,1)S(1)} custom-call(f32[64,320]{1,0:T(8,128)S(1)} %copy-done.1, s32[1,64]{1,0:T(1,128)S(1)} %bitcast.3, s32[1,64]{1,0:T(1,128)S(1)} %bitcast.4, s32[1,64]{1,0:T(1,128)S(1)} %bitcast.5, f32[10,512]{1,0:T(8,128)S(1)} %copy-done.2, bf16[4,3,512,512]{3,2,1,0:T(8,128)(2,1)} %mid_hbm.1, bf16[2,2,512,512]{3,2,1,0:T(8,128)(2,1)S(1)} %copy-done), custom_call_target="tpu_custom_call" | custom-call | tf_op jit(solution)/shard_map/frontend/pallas_call | solution.py:342
  50.4 0.6 %copy.9 = bf16[64,512]{1,0:T(8,128)(2,1)} copy(bf16[64,512]{1,0:T(8,128)(2,1)S(1)} %frontend.1) | data formatting | bytes 131072
Async XLA Ops:
  0.0 1.6 %copy-start = (bf16[2,2,512,512]{3,2,1,0:T(8,128)(2,1)S(1)}, bf16[2,2,512,512]{3,2,1,0:T(8,128)(2,1)}, u32[]{:S(2)}) copy-start(bf16[2,2,512,512]{3,2,1,0:T(8,128)(2,1)} %tail_hbm.1) | copy-start | bytes 6291460
  1.6 0.9 %copy-start.1 = (f32[64,320]{1,0:T(8,128)S(1)}, f32[64,320]{1,0:T(8,128)}, u32[]{:S(2)}) copy-start(f32[64,320]{1,0:T(8,128)} %wave_ref.1) | copy-start | bytes 245764
  2.5 0.8 %copy-start.2 = (f32[10,512]{1,0:T(8,128)S(1)}, f32[10,512]{1,0:T(8,128)}, u32[]{:S(2)}) copy-start(f32[10,512]{1,0:T(8,128)} %first_ref.1) | copy-start | bytes 61444
  3.2 0.7 %copy-start.3 = (s32[64]{0:T(128)S(1)}, s32[64]{0:T(128)}, u32[]{:S(2)}) copy-start(s32[64]{0:T(128)} %param.8) | copy-start | bytes 772
  3.9 0.7 %copy-start.4 = (s32[64]{0:T(128)S(1)}, s32[64]{0:T(128)}, u32[]{:S(2)}) copy-start(s32[64]{0:T(128)} %param.9) | copy-start | bytes 772
  4.6 0.7 %copy-start.5 = (s32[64]{0:T(128)S(1)}, s32[64]{0:T(128)}, u32[]{:S(2)}) copy-start(s32[64]{0:T(128)} %param.10) | copy-start | bytes 772

commit v3 on v2

--- a/solution.py
+++ b/solution.py
@@ -105,7 +105,7 @@
 
 def convs(
     ready, recv_ref, length_ref, trim_ref, first_ref, mid_ref, tail_ref, out_ref,
-    xs, pad, e1, o1, e2, o2, e3, o3, e4, o4, e5, o5, e6, o6, h1, h2, h3, acc,
+    xs, pad, e1, o1, e2, o2, e3, o3, e4, o4, e5, o5, e6, o6, h1, h2, h3, acc, acc2,
 ):
     me = lax.axis_index("dp").astype(F32)
     rows = out_ref.shape[0]
@@ -163,84 +163,105 @@
     h1[:16, :] = norm_gelu(first_dot(halo[:, :16])).astype(BF16).astype(F32)
     h1[16:, :] = jnp.zeros_like(h1[16:, :])
 
-    def first_step(step, carry):
-        where = pl.ds(pl.multiple_of(step * rows, rows), rows)
-        for parity, dest in ((0, e1), (1, o1)):
-            acc[parity * rows : (parity + 1) * rows, :] = first_dot(patches(2 * step + parity)[:, :rows])
+    def pipeline(count, multiply, finish):
+        multiply(0, acc)
+        if count == 1:
+            finish(0, acc)
+            return
+
+        def pair(j, carry):
+            multiply(2 * j + 1, acc2)
+            finish(2 * j, acc)
+            multiply(2 * j + 2, acc)
+            finish(2 * j + 1, acc2)
+            return carry
+
+        if count > 2:
+            lax.fori_loop(0, count // 2 - 1, pair, 0)
+        multiply(count - 1, acc2)
+        finish(count - 2, acc)
+        finish(count - 1, acc2)
+
+    left_half = lax.broadcasted_iota(jnp.int32, (16, 128), 1) < rows
+
+    def first_multiply(step, into):
+        joined = []
+        for index in range(3):
+            even = xs[index, pl.ds(10 * step, 16), :]
+            odd = xs[index, pl.ds(10 * step + 5, 16), :]
+            joined.append(jnp.where(left_half, even, pltpu.roll(odd, rows, 1)))
+        a, b, c = joined
+        into[: 2 * rows, :] = first_dot(jnp.concatenate([a, a, b, b, a, c], axis=0))
+
+    def first_finish(step, source):
         for parity, dest in ((0, e1), (1, o1)):
             for r in range(0, rows, 16):
-                block = acc[parity * rows + r : parity * rows + r + 16, :]
+                block = source[parity * rows + r : parity * rows + r + 16, :]
                 dest[pl.ds(pl.multiple_of(step * rows + r, 16), 16), :] = norm_gelu(block).astype(BF16)
-        return carry
-
-    lax.fori_loop(0, 32, first_step, 0)
+
+    pipeline(32, first_multiply, first_finish)
 
     def wrap(even, halo_ref, phases):
         rolled = pltpu.roll(even[:rows, :].astype(F32), rows - 1, 0)
         shifted = jnp.where(iota(rolled.shape, 0) == rows - 1, halo_ref[0:1, :], rolled)
         even[pl.ds(phases // 2 * rows, rows), :] = shifted.astype(BF16)
 
-    def layer(even, odd, taps, dest_even, dest_odd, phases):
+    def layer(even, odd, weight, count, dest_even, dest_odd, phases):
         chunk = min(phases, 4)
         size = chunk * rows
 
-        def step(index, carry):
-            base = pl.multiple_of(index * size, size)
+        def multiply(index, into):
+            base = index * size
             inputs = [even[pl.ds(base, size), :], odd[pl.ds(base, size), :]]
-            if len(taps) == 3:
-                inputs.append(even[pl.ds(pl.multiple_of(base + rows, rows), size), :])
-            total = None
-            for value, tap in zip(inputs, taps):
-                term = jnp.dot(value, tap[...], preferred_element_type=F32)
-                total = term if total is None else total + term
-            acc[:size, :] = total
+            if count == 3:
+                inputs.append(even[pl.ds(base + rows, size), :])
+            into[:size, :] = jnp.dot(
+                jnp.concatenate(inputs, axis=1), weight[...], preferred_element_type=F32
+            )
+
+        def finish(index, source):
             for p in range(chunk):
                 dest = dest_even if p % 2 == 0 else dest_odd
                 for r in range(0, rows, 16):
-                    block = acc[p * rows + r : p * rows + r + 16, :]
+                    block = source[p * rows + r : p * rows + r + 16, :]
                     at = index * (size // 2) + p // 2 * rows + r
-                    if chunk == 1:
-                        at = r
-                    dest[pl.ds(pl.multiple_of(at, 16), 16), :] = norm_gelu(block).astype(BF16)
-            return carry
-
-        if phases == chunk:
-            step(0, 0)
-        else:
-            lax.fori_loop(0, phases // chunk, step, 0)
-
-    def halo_layer(source, dest, taps):
-        total = None
-        for offset, tap in enumerate(taps):
+                    dest[pl.ds(at, 16), :] = norm_gelu(block).astype(BF16)
+
+        pipeline(phases // chunk, multiply, finish)
+
+    def halo_layer(source, dest, weight):
+        taps = []
+        for offset in range(3):
             choose = jnp.where(iota((16, 24), 1) == 2.0 * iota((16, 24), 0) + offset, 1.0, 0.0)
-            value = jnp.dot(
-                choose.astype(BF16), source[...].astype(BF16), preferred_element_type=F32
-            ).astype(BF16)
-            term = jnp.dot(value, tap[...], preferred_element_type=F32)
-            total = term if total is None else total + term
+            taps.append(
+                jnp.dot(
+                    choose.astype(BF16), source[...].astype(BF16), preferred_element_type=F32
+                ).astype(BF16)
+            )
+        total = jnp.dot(jnp.concatenate(taps, axis=1), weight[...], preferred_element_type=F32)
         dest[:8, :] = norm_gelu(total[:8]).astype(BF16).astype(F32)
         dest[8:, :] = jnp.zeros_like(dest[8:, :])
 
-    mids = [[mid_ref.at[i, t] for t in range(3)] for i in range(4)]
-    tails = [[tail_ref.at[i, t] for t in range(2)] for i in range(2)]
+    mids = [mid_ref.at[i] for i in range(4)]
+    tails = [tail_ref.at[i] for i in range(2)]
     ready(0)
     wrap(e1, h1, 64)
     halo_layer(h1, h2, mids[0])
-    layer(e1, o1, mids[0], e2, o2, 32)
+    layer(e1, o1, mids[0], 3, e2, o2, 32)
     ready(1)
     wrap(e2, h2, 32)
     halo_layer(h2, h3, mids[1])
-    layer(e2, o2, mids[1], e3, o3, 16)
+    layer(e2, o2, mids[1], 3, e3, o3, 16)
     ready(2)
     wrap(e3, h3, 16)
     halo_layer(h3, h1, mids[2])
-    layer(e3, o3, mids[2], e4, o4, 8)
+    layer(e3, o3, mids[2], 3, e4, o4, 8)
     ready(3)
     wrap(e4, h1, 8)
-    layer(e4, o4, mids[3], e5, o5, 4)
+    layer(e4, o4, mids[3], 3, e5, o5, 4)
     ready(4)
-    layer(e5, o5, tails[0], e6, o6, 2)
-    layer(e6, o6, tails[1], out_ref, out_ref, 1)
+    layer(e5, o5, tails[0], 2, e6, o6, 2)
+    layer(e6, o6, tails[1], 2, out_ref, out_ref, 1)
 
 
 def means(n, reach, feature_ref, length_ref, out_ref, send, recv, send_sem, recv_sem):
@@ -333,6 +354,8 @@
     cap = rows // n + 2
     stride = (cap + 1 + 7) // 8 * 8
     reach = min((MAXLEN + rows - 2) // rows, n - 1)
+    mid = mid_weight.reshape(4, 3 * channels, channels)
+    tail = tail_weight.reshape(2, 2 * channels, channels)
     vmem = pl.BlockSpec(memory_space=pltpu.VMEM)
     outside = pl.BlockSpec(memory_space=pl.ANY)
 
@@ -350,8 +373,8 @@
             pltpu.VMEM((n * stride, WIDE), F32),
             pltpu.SemaphoreType.DMA((n,)),
             pltpu.SemaphoreType.DMA((n,)),
-            pltpu.VMEM(mid_weight.shape, BF16),
-            pltpu.VMEM(tail_weight.shape, BF16),
+            pltpu.VMEM(mid.shape, BF16),
+            pltpu.VMEM(tail.shape, BF16),
             pltpu.SemaphoreType.DMA((5,)),
             pltpu.VMEM((rows, channels), BF16),
             pltpu.VMEM((2, 8, 128), F32),
@@ -366,6 +389,7 @@
             pltpu.VMEM((24, channels), F32),
             pltpu.VMEM((24, channels), F32),
             pltpu.VMEM((4 * rows, channels), F32),
+            pltpu.VMEM((4 * rows, channels), F32),
         ],
         compiler_params=pltpu.CompilerParams(
             collective_id=0, has_side_effects=True, vmem_limit_bytes=48 * 1024 * 1024
@@ -373,7 +397,7 @@
         name="frontend",
     )(
         wave, row_slot.reshape(1, -1), frame_lengths.reshape(1, -1), sample_trim.reshape(1, -1),
-        first_weight, mid_weight, tail_weight,
+        first_weight, mid, tail,
     )
 
 

time: 51.3 us -> 41.4 us (0.81)
  Pallas kernels: 45.1 us -> 35.3 us
    pallas_call x1, Pallas kernels: 45.1 us -> 35.3 us  [per_device(): pl.pallas_call(functools.partial(frontend_kernel, n, cap, stride, reach),...]
where the time goes in v3:
time: 41.4 us; the launch traced here: 41.1 us
  Pallas kernels  35.3 us (85%)
  local copies, waits for them, and re-layouts  5.84 us (14%)
    pallas_call x1, Pallas kernels, per_device(): pl.pallas_call(functools.partial(frontend_kernel, n, cap, stride, reach),...  35.3 us
    unnamed x13, local copies, waits for them, and re-layouts  5.84 us

profile of v3, /device:TPU:0, one launch (start us, length us, event | category | flops | bytes accessed | tf_op | source)
XLA Modules:
  0.0 41.1 jit_solution(212367940182954762)
XLA Ops:
  0.0 0.0 copy-start
  0.0 1.6 %copy-done = bf16[2,2,512,512]{3,2,1,0:T(8,128)(2,1)S(1)} copy-done((bf16[2,2,512,512]{3,2,1,0:T(8,128)(2,1)S(1)}, bf16[2,2,512,512]{3,2,1,0:T(8,128)(2,1)}, u32[]{:S(2)}) %copy-start) | copy-done | bytes 2097176
  1.6 0.0 copy-start.1
  1.6 0.9 %copy-done.1 = f32[64,320]{1,0:T(8,128)S(1)} copy-done((f32[64,320]{1,0:T(8,128)S(1)}, f32[64,320]{1,0:T(8,128)}, u32[]{:S(2)}) %copy-start.1) | copy-done | bytes 81944
  2.5 0.0 copy-start.2
  2.5 0.8 %copy-done.2 = f32[10,512]{1,0:T(8,128)S(1)} copy-done((f32[10,512]{1,0:T(8,128)S(1)}, f32[10,512]{1,0:T(8,128)}, u32[]{:S(2)}) %copy-start.2) | copy-done | bytes 20504
  3.2 0.0 copy-start.3
  3.2 0.7 %copy-done.3 = s32[64]{0:T(128)S(1)} copy-done((s32[64]{0:T(128)S(1)}, s32[64]{0:T(128)}, u32[]{:S(2)}) %copy-start.3) | copy-done | bytes 280
  3.9 0.0 copy-start.4
  3.9 0.7 %copy-done.4 = s32[64]{0:T(128)S(1)} copy-done((s32[64]{0:T(128)S(1)}, s32[64]{0:T(128)}, u32[]{:S(2)}) %copy-start.4) | copy-done | bytes 280
  4.6 0.0 copy-start.5
  4.6 0.7 %copy-done.5 = s32[64]{0:T(128)S(1)} copy-done((s32[64]{0:T(128)S(1)}, s32[64]{0:T(128)}, u32[]{:S(2)}) %copy-start.5) | copy-done | bytes 280
  5.2 35.3 %frontend.1 = bf16[64,512]{1,0:T(8,128)(2,1)S(1)} custom-call(f32[64,320]{1,0:T(8,128)S(1)} %copy-done.1, s32[1,64]{1,0:T(1,128)S(1)} %bitcast.6, s32[1,64]{1,0:T(1,128)S(1)} %bitcast.7, s32[1,64]{1,0:T(1,128)S(1)} %bitcast.8, f32[10,512]{1,0:T(8,128)S(1)} %copy-done.2, bf16[4,1536,512]{2,1,0:T(8,128)(2,1)} %bitcast.9, bf16[2,1024,512]{2,1,0:T(8,128)(2,1)S(1)} %bitcast.5), custom_call_target="tpu_custom_call" | custom-call | tf_op jit(solution)/shard_map/frontend/pallas_call | solution.py:365
  40.5 0.6 %copy.9 = bf16[64,512]{1,0:T(8,128)(2,1)} copy(bf16[64,512]{1,0:T(8,128)(2,1)S(1)} %frontend.1) | data formatting | bytes 131072
Async XLA Ops:
  0.0 1.6 %copy-start = (bf16[2,2,512,512]{3,2,1,0:T(8,128)(2,1)S(1)}, bf16[2,2,512,512]{3,2,1,0:T(8,128)(2,1)}, u32[]{:S(2)}) copy-start(bf16[2,2,512,512]{3,2,1,0:T(8,128)(2,1)} %param.13) | copy-start | bytes 6291460
  1.6 0.9 %copy-start.1 = (f32[64,320]{1,0:T(8,128)S(1)}, f32[64,320]{1,0:T(8,128)}, u32[]{:S(2)}) copy-start(f32[64,320]{1,0:T(8,128)} %wave_ref.1) | copy-start | bytes 245764
  2.5 0.8 %copy-start.2 = (f32[10,512]{1,0:T(8,128)S(1)}, f32[10,512]{1,0:T(8,128)}, u32[]{:S(2)}) copy-start(f32[10,512]{1,0:T(8,128)} %first_ref.1) | copy-start | bytes 61444
  3.2 0.7 %copy-start.3 = (s32[64]{0:T(128)S(1)}, s32[64]{0:T(128)}, u32[]{:S(2)}) copy-start(s32[64]{0:T(128)} %param.8) | copy-start | bytes 772
  3.9 0.7 %copy-start.4 = (s32[64]{0:T(128)S(1)}, s32[64]{0:T(128)}, u32[]{:S(2)}) copy-start(s32[64]{0:T(128)} %param.9) | copy-start | bytes 772
  4.6 0.7 %copy-start.5 = (s32[64]{0:T(128)S(1)}, s32[64]{0:T(128)}, u32[]{:S(2)}) copy-start(s32[64]{0:T(128)} %param.10) | copy-start | bytes 772

commit v4 on v3

--- a/solution.py
+++ b/solution.py
@@ -35,7 +35,10 @@
 
 def norm_gelu(values):
     average = jnp.mean(values, axis=-1, keepdims=True)
-    centred = values - average
+    return scale_gelu(values - average)
+
+
+def scale_gelu(centred):
     spread = jnp.mean(centred * centred, axis=-1, keepdims=True)
     scaled = centred * (lax.rsqrt(spread + EPS) * HALF_ROOT)
     half = scaled * HALF_ROOT
@@ -138,7 +141,7 @@
 
     pad[...] = jnp.zeros_like(pad)
     pad[: first_ref.shape[0], :] = first_ref[...]
-    first = pad[...]
+    first = pad[...] - jnp.mean(pad[...], axis=-1, keepdims=True)
     weight1 = first.astype(BF16).astype(F32)
     left = first - weight1
     weight2 = left.astype(BF16).astype(F32)
@@ -160,7 +163,7 @@
         )
 
     halo = lax.fori_loop(0, 16, gather_halo, jnp.zeros((96, 128), F32))
-    h1[:16, :] = norm_gelu(first_dot(halo[:, :16])).astype(BF16).astype(F32)
+    h1[:16, :] = scale_gelu(first_dot(halo[:, :16])).astype(BF16).astype(F32)
     h1[16:, :] = jnp.zeros_like(h1[16:, :])
 
     def pipeline(count, multiply, finish):
@@ -197,7 +200,7 @@
         for parity, dest in ((0, e1), (1, o1)):
             for r in range(0, rows, 16):
                 block = source[parity * rows + r : parity * rows + r + 16, :]
-                dest[pl.ds(pl.multiple_of(step * rows + r, 16), 16), :] = norm_gelu(block).astype(BF16)
+                dest[pl.ds(pl.multiple_of(step * rows + r, 16), 16), :] = scale_gelu(block).astype(BF16)
 
     pipeline(32, first_multiply, first_finish)
 

time: 41.4 us -> 39.8 us (0.961)
  Pallas kernels: 35.3 us -> 33.7 us
    pallas_call x1, Pallas kernels: 35.3 us -> 33.7 us  [per_device(): pl.pallas_call(functools.partial(frontend_kernel, n, cap, stride, reach),...]
where the time goes in v4:
time: 39.8 us; the launch traced here: 39.5 us
  Pallas kernels  33.7 us (85%)
  local copies, waits for them, and re-layouts  5.84 us (15%)
    pallas_call x1, Pallas kernels, per_device(): pl.pallas_call(functools.partial(frontend_kernel, n, cap, stride, reach),...  33.7 us
    unnamed x13, local copies, waits for them, and re-layouts  5.84 us

profile of v4, /device:TPU:0, one launch (start us, length us, event | category | flops | bytes accessed | tf_op | source)
XLA Modules:
  0.0 39.5 jit_solution(9824883519512215225)
XLA Ops:
  0.0 0.0 copy-start
  0.0 1.6 %copy-done = bf16[2,2,512,512]{3,2,1,0:T(8,128)(2,1)S(1)} copy-done((bf16[2,2,512,512]{3,2,1,0:T(8,128)(2,1)S(1)}, bf16[2,2,512,512]{3,2,1,0:T(8,128)(2,1)}, u32[]{:S(2)}) %copy-start) | copy-done | bytes 2097176
  1.6 0.0 copy-start.1
  1.6 0.9 %copy-done.1 = f32[64,320]{1,0:T(8,128)S(1)} copy-done((f32[64,320]{1,0:T(8,128)S(1)}, f32[64,320]{1,0:T(8,128)}, u32[]{:S(2)}) %copy-start.1) | copy-done | bytes 81944
  2.5 0.0 copy-start.2
  2.5 0.8 %copy-done.2 = f32[10,512]{1,0:T(8,128)S(1)} copy-done((f32[10,512]{1,0:T(8,128)S(1)}, f32[10,512]{1,0:T(8,128)}, u32[]{:S(2)}) %copy-start.2) | copy-done | bytes 20504
  3.2 0.0 copy-start.3
  3.2 0.7 %copy-done.3 = s32[64]{0:T(128)S(1)} copy-done((s32[64]{0:T(128)S(1)}, s32[64]{0:T(128)}, u32[]{:S(2)}) %copy-start.3) | copy-done | bytes 280
  3.9 0.0 copy-start.4
  3.9 0.7 %copy-done.4 = s32[64]{0:T(128)S(1)} copy-done((s32[64]{0:T(128)S(1)}, s32[64]{0:T(128)}, u32[]{:S(2)}) %copy-start.4) | copy-done | bytes 280
  4.6 0.0 copy-start.5
  4.6 0.7 %copy-done.5 = s32[64]{0:T(128)S(1)} copy-done((s32[64]{0:T(128)S(1)}, s32[64]{0:T(128)}, u32[]{:S(2)}) %copy-start.5) | copy-done | bytes 280
  5.2 33.7 %frontend.1 = bf16[64,512]{1,0:T(8,128)(2,1)S(1)} custom-call(f32[64,320]{1,0:T(8,128)S(1)} %copy-done.1, s32[1,64]{1,0:T(1,128)S(1)} %bitcast.6, s32[1,64]{1,0:T(1,128)S(1)} %bitcast.7, s32[1,64]{1,0:T(1,128)S(1)} %bitcast.8, f32[10,512]{1,0:T(8,128)S(1)} %copy-done.2, bf16[4,1536,512]{2,1,0:T(8,128)(2,1)} %bitcast.9, bf16[2,1024,512]{2,1,0:T(8,128)(2,1)S(1)} %bitcast.5), custom_call_target="tpu_custom_call" | custom-call | tf_op jit(solution)/shard_map/frontend/pallas_call | solution.py:368
  38.9 0.6 %copy.9 = bf16[64,512]{1,0:T(8,128)(2,1)} copy(bf16[64,512]{1,0:T(8,128)(2,1)S(1)} %frontend.1) | data formatting | bytes 131072
Async XLA Ops:
  0.0 1.6 %copy-start = (bf16[2,2,512,512]{3,2,1,0:T(8,128)(2,1)S(1)}, bf16[2,2,512,512]{3,2,1,0:T(8,128)(2,1)}, u32[]{:S(2)}) copy-start(bf16[2,2,512,512]{3,2,1,0:T(8,128)(2,1)} %param.13) | copy-start | bytes 6291460
  1.6 0.9 %copy-start.1 = (f32[64,320]{1,0:T(8,128)S(1)}, f32[64,320]{1,0:T(8,128)}, u32[]{:S(2)}) copy-start(f32[64,320]{1,0:T(8,128)} %wave_ref.1) | copy-start | bytes 245764
  2.5 0.8 %copy-start.2 = (f32[10,512]{1,0:T(8,128)S(1)}, f32[10,512]{1,0:T(8,128)}, u32[]{:S(2)}) copy-start(f32[10,512]{1,0:T(8,128)} %first_ref.1) | copy-start | bytes 61444
  3.2 0.7 %copy-start.3 = (s32[64]{0:T(128)S(1)}, s32[64]{0:T(128)}, u32[]{:S(2)}) copy-start(s32[64]{0:T(128)} %param.8) | copy-start | bytes 772
  3.9 0.7 %copy-start.4 = (s32[64]{0:T(128)S(1)}, s32[64]{0:T(128)}, u32[]{:S(2)}) copy-start(s32[64]{0:T(128)} %param.9) | copy-start | bytes 772
  4.6 0.7 %copy-start.5 = (s32[64]{0:T(128)S(1)}, s32[64]{0:T(128)}, u32[]{:S(2)}) copy-start(s32[64]{0:T(128)} %param.10) | copy-start | bytes 772
